TPU v7x, 512 devices: a whole 4x8x8 slice. The times are simulated.
512 devices in a mesh: edp: 16 (over z, core), ep: 32 (over y, x).
Axes of the slice: x: 4, y: 8, z: 8, core: 2. Of those that a mesh axis runs over, the one named last changes fastest.
Arguments:
- token_acts: bfloat16 [16, 32, 2, 64, 1024], P('edp', 'ep'), may hold values from -6 to 6
- out_grad: bfloat16 [16, 32, 3584, 128], P('edp', 'ep'), may hold values from -0.59765625 to 0.59765625
- counts: int32 [16, 32, 2], P('edp', 'ep'), may hold values from 1 to 64, as said below
- params: float32 [32, 3584, 1024], P('ep', 'edp'), may hold values from -3 to 3
- first_moment: bfloat16 [32, 3584, 1024], P('ep', 'edp'), may hold values from -3 to 3
- second_moment: bfloat16 [32, 3584, 1024], P('ep', 'edp'), may hold values from 0.049804688 to 2
- old_expert: int32 [32], replicated, may hold values from 0 to 31, each once
- replica_of: int32 [32], replicated, may hold values from 0 to 31
- new_expert: int32 [32], replicated, may hold values from 0 to 31, each once
Outputs:
- update_step: float32 [32, 3584, 1024], P('ep', 'edp')
- new_first: bfloat16 [32, 3584, 1024], P('ep', 'edp')
- new_second: bfloat16 [32, 3584, 1024], P('ep', 'edp')
Inputs may be any that keep to these rules, and one draw needn't show every extreme that they name: `counts`: every slot has at least one live token; some slot is full and some slot has exactly one live token in every draw. `old_expert`: each expert appears exactly once. `new_expert`: each expert appears exactly once. `replica_of`: any expert may be served by any number of replica slots, its owner's included.
All inputs are finite; a program needn't handle non-finite values.
Results may differ from a plain program's by a relative error of at most 0.015.
Values may be sent and summed in bfloat16 or wider, within the bound.
A program may use at most 64 MiB of HBM per device.

v0:
```python
import jax
import jax.numpy as jnp
from jax import lax
from jax.sharding import PartitionSpec as P

beta_one = 0.9
beta_two = 0.95
bias_one = 0.9999734386011124
bias_two = 0.994079470779666
decay_rate = 0.1
adam_eps = 1e-08


def adam_update(weights, first_old, second_old, gradient):
    first_new = beta_one * first_old.astype(jnp.float32) + (1.0 - beta_one) * gradient
    second_new = beta_two * second_old.astype(jnp.float32) + (1.0 - beta_two) * gradient * gradient
    scaled = first_new / bias_one / (jnp.sqrt(second_new / bias_two) + adam_eps)
    step_new = -(scaled + decay_rate * weights)
    return (step_new, first_new.astype(jnp.bfloat16), second_new.astype(jnp.bfloat16))


def local(
    token_acts,
    out_grad,
    counts,
    params,
    first_moment,
    second_moment,
    old_expert,
    replica_of,
    new_expert,
):
    groups = lax.axis_size("edp")
    owners = lax.axis_size("ep")
    model_width = out_grad.shape[2]
    slot_count = token_acts.shape[2]
    tok_slot = token_acts.shape[3]
    hidden_units = token_acts.shape[4]
    row_count = model_width // groups
    piece_len = row_count * hidden_units // owners
    local_grad = out_grad[0, 0]
    local_counts = counts[0, 0]
    column = jnp.arange(slot_count * tok_slot, dtype=jnp.int32)
    slot_index = column // tok_slot
    live_limit = jnp.where(slot_index == 0, local_counts[0], local_counts[1])
    live_mask = column % tok_slot < live_limit
    masked = jnp.where(live_mask[None, :], local_grad, jnp.zeros_like(local_grad))
    received = lax.all_to_all(
        masked.reshape(groups, row_count, slot_count * tok_slot),
        "edp",
        split_axis=0,
        concat_axis=0,
        tiled=True,
    )
    arrived = lax.all_gather(token_acts[0], "edp", axis=0, tiled=True)
    count_here = arrived.shape[0]
    grad_block = received
    grad_block = grad_block.reshape(count_here, row_count, slot_count, tok_slot)
    slot_grads = jnp.einsum(
        "adst,astf->sdf", grad_block, arrived, preferred_element_type=jnp.float32
    )
    own_grad = slot_grads[0].reshape(owners, piece_len)
    replica_grad = slot_grads[1].reshape(owners, piece_len)
    sum_matrix = (replica_of[None, :] == old_expert[:, None]).astype(jnp.float32)
    move_matrix = (old_expert[None, :] == new_expert[:, None]).astype(jnp.float32)
    weights = params[0].reshape(owners, piece_len)
    first_old = first_moment[0].reshape(owners, piece_len)
    second_old = second_moment[0].reshape(owners, piece_len)
    replica_sent = lax.all_to_all(
        replica_grad.astype(jnp.bfloat16), "ep", split_axis=0, concat_axis=0, tiled=True
    ).astype(replica_grad.dtype)
    set_sums = jnp.dot(sum_matrix, replica_sent, precision=lax.Precision.HIGHEST)
    returned = lax.all_to_all(
        set_sums.astype(jnp.bfloat16), "ep", split_axis=0, concat_axis=0, tiled=True
    ).astype(set_sums.dtype)
    weights, first_old, second_old = adam_update(
        weights, first_old, second_old, own_grad + returned
    )
    weight_pieces = lax.all_to_all(weights, "ep", split_axis=0, concat_axis=0, tiled=True)
    first_pieces, second_pieces = (
        lax.all_to_all(first_old, "ep", split_axis=0, concat_axis=0, tiled=True),
        lax.all_to_all(second_old, "ep", split_axis=0, concat_axis=0, tiled=True),
    )
    placed_steps = jnp.dot(move_matrix, weight_pieces, precision=lax.Precision.HIGHEST)
    move_half = move_matrix.astype(jnp.bfloat16)
    placed_first = jnp.dot(move_half, first_pieces, preferred_element_type=jnp.float32).astype(
        jnp.bfloat16
    )
    placed_second = jnp.dot(move_half, second_pieces, preferred_element_type=jnp.float32).astype(
        jnp.bfloat16
    )
    final_steps = lax.all_to_all(placed_steps, "ep", split_axis=0, concat_axis=0, tiled=True)
    final_first, final_second = (
        lax.all_to_all(placed_first, "ep", split_axis=0, concat_axis=0, tiled=True),
        lax.all_to_all(placed_second, "ep", split_axis=0, concat_axis=0, tiled=True),
    )
    return (
        final_steps.reshape(1, row_count, hidden_units),
        final_first.reshape(1, row_count, hidden_units),
        final_second.reshape(1, row_count, hidden_units),
    )


def solution(mesh):
    return jax.shard_map(
        local,
        mesh=mesh,
        in_specs=(
            P("edp", "ep", None, None, None),
            P("edp", "ep", None, None),
            P("edp", "ep", None),
            P("ep", "edp", None),
            P("ep", "edp", None),
            P("ep", "edp", None),
            P(),
            P(),
            P(),
        ),
        out_specs=(P("ep", "edp", None), P("ep", "edp", None), P("ep", "edp", None)),
        check_vma=False,
    )
```

profile of v0, /device:TPU:6, one launch (start us, length us, event | category | flops | bytes accessed | tf_op | source)
XLA Modules:
  0.0 280.2 jit_solution(12393630941862970195)
XLA Ops:
  11.8 41.0 %all_to_all.77 = bf16[16,224,128]{2,1,0:T(8,128)(2,1)S(1)} all-to-all(bf16[16,224,128]{2,1,0:T(8,128)(2,1)S(1)} %broadcast_select_fusion), channel_id=1, replica_groups=mesh['edp'=16,'ep'=32] {'edp'}, dimensions={0} | all-to-all | bytes 1835008 | tf_op jit(solution)/shard_map/all_to_all | solution.py:48
  53.3 18.0 %all-gather.3.cloned.1.call-done = bf16[16,1,2,64,1024]{4,3,2,1,0:T(8,128)(2,1)} async-done(((bf16[1,1,2,64,1024]{4,3,2,1,0:T(8,128)(2,1)}), bf16[16,1,2,64,1024]{4,3,2,1,0:T(8,128)(2,1)}) %all-gather.3.cloned.1.call-update) | async-done | bytes 4194320 | tf_op jit(solution)/shard_map/all_gather | solution.py:55
  71.3 3.3 %fusion.5 = f32[2,224,1024]{2,1,0:T(8,128)S(1)} fusion(bf16[16,224,2,64]{1,3,2,0:T(8,128)(2,1)S(1)} %bitcast.32, bf16[16,1,2,64,1024]{4,3,2,1,0:T(8,128)(2,1)} %all-gather.3.cloned.1.call-done), kind=kOutput, calls=%fused_computation.9 | convolution fusion | flops 939524096 | bytes 6946816 | tf_op jit(solution)/shard_map/adst,astf->sdf/dot_general | solution.py:59
  75.6 3.3 %reduce.3 = bf16[32,7168]{1,0:T(8,128)(2,1)S(1)} reduce(bf16[32,1,7168]{2,1,0:T(2,128)(2,1)S(1)} %convert_element_type.77, bf16[]{:T(256)} %broadcast.125), dimensions={1}, to_apply=%convert_element_type.77.reduce_sub_computation | reduce | bytes 917506 | tf_op jit(solution)/shard_map/convert_element_type | solution.py:70
  79.3 25.8 %all_to_all.78 = bf16[32,2,3584]{2,1,0:T(2,128)(2,1)S(1)} all-to-all(bf16[32,2,3584]{2,1,0:T(2,128)(2,1)S(1)} %reshape.144), channel_id=1, replica_groups=mesh['edp'=16,'ep'=32] {'ep'}, dimensions={0} | all-to-all | bytes 917504 | tf_op jit(solution)/shard_map/all_to_all | solution.py:69
  107.8 5.6 %all-to-all-start.2 = ((bf16[32,2,3584]{2,1,0:T(2,128)(2,1)}), bf16[32,2,3584]{2,1,0:T(2,128)(2,1)S(1)}, u32[]{:S(2)}, u32[]{:S(2)}) async-start(bf16[32,2,3584]{2,1,0:T(2,128)(2,1)} %reshape.146), calls=%async_computation.2 | async-start | bytes 917504 | tf_op jit(solution)/shard_map/all_to_all | solution.py:73
  113.4 2.2 broadcast_multiply_fusion
  119.2 2.6 mul.67
  123.9 2.5 mul.71
  130.1 3.1 %fusion.32 = (bf16[32,1,7168]{2,0,1:T(8,128)(2,1)}, f32[32,1,7168]{2,0,1:T(8,128)S(1)}, bf16[32,1,7168]{2,0,1:T(8,128)(2,1)S(1)}) fusion(f32[32,1,7168]{2,0,1:T(8,128)} %mul.71, f32[32,1,7168]{2,0,1:T(8,128)S(1)} %reshape_squeeze.2, bf16[32,1,7168]{2,1,0:T(2,128)(2,1)} %reshape.147, f32[32,1,7168]{2,0,1:T(8,128)S(1)} %mul.76, f32[32,1,7168]{2,0,1:T(8,128)} %mul.67), kind=kLoop, calls=%fused_computation.47 | loop fusion | flops 3440640 | bytes 5963776 | tf_op jit(solution)/shard_map/convert_element_type | solution.py:19
  136.2 9.8 %all-to-all-start.7 = ((bf16[32,2,3584]{2,1,0:T(2,128)(2,1)}), bf16[32,2,3584]{2,1,0:T(2,128)(2,1)S(1)}, u32[]{:S(2)}, u32[]{:S(2)}) async-start(bf16[32,2,3584]{2,1,0:T(2,128)(2,1)} %reshape.152), calls=%async_computation.7 | async-start | bytes 917504 | tf_op jit(solution)/shard_map/all_to_all | solution.py:82
  148.0 12.1 %all-to-all-done.7 = bf16[32,2,3584]{2,1,0:T(2,128)(2,1)S(1)} async-done(((bf16[32,2,3584]{2,1,0:T(2,128)(2,1)}), bf16[32,2,3584]{2,1,0:T(2,128)(2,1)S(1)}, u32[]{:S(2)}, u32[]{:S(2)}) %all-to-all-start.7) | async-done | bytes 458784 | tf_op jit(solution)/shard_map/all_to_all | solution.py:82
  160.1 5.7 %all-to-all-start.5 = ((bf16[32,2,3584]{2,1,0:T(2,128)(2,1)}), bf16[32,2,3584]{2,1,0:T(2,128)(2,1)S(1)}, u32[]{:S(2)}, u32[]{:S(2)}) async-start(bf16[32,2,3584]{2,1,0:T(2,128)(2,1)} %reshape.148), calls=%async_computation.5 | async-start | bytes 917504 | tf_op jit(solution)/shard_map/all_to_all | solution.py:81
  168.5 10.7 %all-to-all-done.5 = bf16[32,2,3584]{2,1,0:T(2,128)(2,1)S(1)} async-done(((bf16[32,2,3584]{2,1,0:T(2,128)(2,1)}), bf16[32,2,3584]{2,1,0:T(2,128)(2,1)S(1)}, u32[]{:S(2)}, u32[]{:S(2)}) %all-to-all-start.5) | async-done | bytes 458784 | tf_op jit(solution)/shard_map/all_to_all | solution.py:81
  179.2 5.6 %all-to-all-start.8 = ((bf16[32,2,3584]{2,1,0:T(2,128)(2,1)}), bf16[32,2,3584]{2,1,0:T(2,128)(2,1)S(1)}, u32[]{:S(2)}, u32[]{:S(2)}) async-start(bf16[32,2,3584]{2,1,0:T(2,128)(2,1)} %reshape.154), calls=%async_computation.8 | async-start | bytes 917504 | tf_op jit(solution)/shard_map/all_to_all | solution.py:95
  186.7 11.1 %all-to-all-done.8 = bf16[32,2,3584]{2,1,0:T(2,128)(2,1)S(1)} async-done(((bf16[32,2,3584]{2,1,0:T(2,128)(2,1)}), bf16[32,2,3584]{2,1,0:T(2,128)(2,1)S(1)}, u32[]{:S(2)}, u32[]{:S(2)}) %all-to-all-start.8) | async-done | bytes 458784 | tf_op jit(solution)/shard_map/all_to_all | solution.py:95
  197.8 5.6 %all-to-all-start.3 = ((f32[32,1,7168]{2,1,0:T(1,128)}), f32[32,1,7168]{2,1,0:T(1,128)S(1)}, u32[]{:S(2)}, u32[]{:S(2)}) async-start(f32[32,1,7168]{2,1,0:T(1,128)} %copy.35), calls=%async_computation.3 | async-start | bytes 1835008 | tf_op jit(solution)/shard_map/all_to_all | solution.py:79
  206.0 19.8 %all-to-all-done.3 = f32[32,1,7168]{2,1,0:T(1,128)S(1)} async-done(((f32[32,1,7168]{2,1,0:T(1,128)}), f32[32,1,7168]{2,1,0:T(1,128)S(1)}, u32[]{:S(2)}, u32[]{:S(2)}) %all-to-all-start.3) | async-done | bytes 917536 | tf_op jit(solution)/shard_map/all_to_all | solution.py:79
  225.8 5.6 %all-to-all-start.6 = ((bf16[32,2,3584]{2,1,0:T(2,128)(2,1)}), bf16[32,2,3584]{2,1,0:T(2,128)(2,1)S(1)}, u32[]{:S(2)}, u32[]{:S(2)}) async-start(bf16[32,2,3584]{2,1,0:T(2,128)(2,1)} %reshape.150), calls=%async_computation.6 | async-start | bytes 917504 | tf_op jit(solution)/shard_map/all_to_all | solution.py:94
  233.9 9.8 %all-to-all-done.6 = bf16[32,2,3584]{2,1,0:T(2,128)(2,1)S(1)} async-done(((bf16[32,2,3584]{2,1,0:T(2,128)(2,1)}), bf16[32,2,3584]{2,1,0:T(2,128)(2,1)S(1)}, u32[]{:S(2)}, u32[]{:S(2)}) %all-to-all-start.6) | async-done | bytes 458784 | tf_op jit(solution)/shard_map/all_to_all | solution.py:94
  243.7 5.6 %all-to-all-start.4 = ((f32[32,1,7168]{2,1,0:T(1,128)}), f32[32,1,7168]{2,1,0:T(1,128)S(1)}, u32[]{:S(2)}, u32[]{:S(2)}) async-start(f32[32,1,7168]{2,1,0:T(1,128)} %copy.36), calls=%async_computation.4 | async-start | bytes 1835008 | tf_op jit(solution)/shard_map/all_to_all | solution.py:92
  249.6 2.7 reduce.2
  254.0 2.7 reduce.1
  258.0 12.1 %all-to-all-done.4 = f32[32,1,7168]{2,1,0:T(1,128)S(1)} async-done(((f32[32,1,7168]{2,1,0:T(1,128)}), f32[32,1,7168]{2,1,0:T(1,128)S(1)}, u32[]{:S(2)}, u32[]{:S(2)}) %all-to-all-start.4) | async-done | bytes 917536 | tf_op jit(solution)/shard_map/all_to_all | solution.py:92
  (48 shorter events, 39.6 us)
Async XLA Ops:
  7.2 64.1 %all-gather.3.cloned.1.call-start = ((), (), s32[]{:S(2)}) async-start(), calls=%async_computation.9 | async-start | bytes 4456448 | tf_op jit(solution)/shard_map/all_gather | solution.py:55
  74.6 30.8 %copy-start = (s32[32]{0:T(128)S(1)}, s32[32]{0:T(128)}, u32[]{:S(2)}) copy-start(s32[32]{0:T(128)} %param.15) | copy-start | bytes 388
  74.7 30.8 %copy-start.2 = (s32[32]{0:T(128)S(1)}, s32[32]{0:T(128)}, u32[]{:S(2)}) copy-start(s32[32]{0:T(128)} %param.16) | copy-start | bytes 388
  107.8 21.2 %all-to-all-start.2 = ((bf16[32,2,3584]{2,1,0:T(2,128)(2,1)}), bf16[32,2,3584]{2,1,0:T(2,128)(2,1)S(1)}, u32[]{:S(2)}, u32[]{:S(2)}) async-start(bf16[32,2,3584]{2,1,0:T(2,128)(2,1)} %reshape.146), calls=%async_computation.2 | async-start | bytes 917504 | tf_op jit(solution)/shard_map/all_to_all | solution.py:73
  133.2 33.0 %copy-start.1 = (s32[32]{0:T(128)S(1)}, s32[32]{0:T(128)}, u32[]{:S(2)}) copy-start(s32[32]{0:T(128)} %param.17) | copy-start | bytes 388
  136.2 23.9 %all-to-all-start.7 = ((bf16[32,2,3584]{2,1,0:T(2,128)(2,1)}), bf16[32,2,3584]{2,1,0:T(2,128)(2,1)S(1)}, u32[]{:S(2)}, u32[]{:S(2)}) async-start(bf16[32,2,3584]{2,1,0:T(2,128)(2,1)} %reshape.152), calls=%async_computation.7 | async-start | bytes 917504 | tf_op jit(solution)/shard_map/all_to_all | solution.py:82
  160.1 19.2 %all-to-all-start.5 = ((bf16[32,2,3584]{2,1,0:T(2,128)(2,1)}), bf16[32,2,3584]{2,1,0:T(2,128)(2,1)S(1)}, u32[]{:S(2)}, u32[]{:S(2)}) async-start(bf16[32,2,3584]{2,1,0:T(2,128)(2,1)} %reshape.148), calls=%async_computation.5 | async-start | bytes 917504 | tf_op jit(solution)/shard_map/all_to_all | solution.py:81
  179.2 18.6 %all-to-all-start.8 = ((bf16[32,2,3584]{2,1,0:T(2,128)(2,1)}), bf16[32,2,3584]{2,1,0:T(2,128)(2,1)S(1)}, u32[]{:S(2)}, u32[]{:S(2)}) async-start(bf16[32,2,3584]{2,1,0:T(2,128)(2,1)} %reshape.154), calls=%async_computation.8 | async-start | bytes 917504 | tf_op jit(solution)/shard_map/all_to_all | solution.py:95
  197.8 28.0 %all-to-all-start.3 = ((f32[32,1,7168]{2,1,0:T(1,128)}), f32[32,1,7168]{2,1,0:T(1,128)S(1)}, u32[]{:S(2)}, u32[]{:S(2)}) async-start(f32[32,1,7168]{2,1,0:T(1,128)} %copy.35), calls=%async_computation.3 | async-start | bytes 1835008 | tf_op jit(solution)/shard_map/all_to_all | solution.py:79
  225.8 17.8 %all-to-all-start.6 = ((bf16[32,2,3584]{2,1,0:T(2,128)(2,1)}), bf16[32,2,3584]{2,1,0:T(2,128)(2,1)S(1)}, u32[]{:S(2)}, u32[]{:S(2)}) async-start(bf16[32,2,3584]{2,1,0:T(2,128)(2,1)} %reshape.150), calls=%async_computation.6 | async-start | bytes 917504 | tf_op jit(solution)/shard_map/all_to_all | solution.py:94
  243.7 26.5 %all-to-all-start.4 = ((f32[32,1,7168]{2,1,0:T(1,128)}), f32[32,1,7168]{2,1,0:T(1,128)S(1)}, u32[]{:S(2)}, u32[]{:S(2)}) async-start(f32[32,1,7168]{2,1,0:T(1,128)} %copy.36), calls=%async_computation.4 | async-start | bytes 1835008 | tf_op jit(solution)/shard_map/all_to_all | solution.py:92
Sparse Core Ops, SparseCore 0:
  10.1 61.1 all-gather.2
where the time goes:
time: 282 us; the launch traced here: 280 us
  waiting for transfers between devices  94.3 us (33%)
  blocking collectives  66.8 us (24%)
  starting transfers between devices  43.4 us (15%)
  local copies, waits for them, and re-layouts  28.2 us (10%)
  other arithmetic  28.2 us (10%)
  between operations  14.3 us (5%)
  matrix products  4.96 us (2%)
    all_to_all x1, blocking collectives, local(): lax.all_to_all(masked.reshape(groups, row_count, slot_count * tok_slot),...  41 us
    all_to_all x1, blocking collectives, local(): lax.all_to_all(replica_grad.astype(jnp.bfloat16), 'ep', split_axis=0, con...  25.8 us
    all_to_all x1, waiting for transfers between devices, local(): lax.all_to_all(weights, 'ep', split_axis=0, concat_axis=0, tiled=True)  19.8 us
    all_gather x1, waiting for transfers between devices, local(): arrived = lax.all_gather(token_acts[0], 'edp', axis=0, tiled=True)  18 us
    all_to_all x1, waiting for transfers between devices, local(): lax.all_to_all(second_old, 'ep', split_axis=0, concat_axis=0, tiled=True)  12.1 us
    all_to_all x1, waiting for transfers between devices, local(): lax.all_to_all(placed_steps, 'ep', split_axis=0, concat_axis=0, tiled=True)  12.1 us
    all_to_all x1, waiting for transfers between devices, local(): lax.all_to_all(placed_second, 'ep', split_axis=0, concat_axis=0, tiled=True)  11.1 us
    all_to_all x1, waiting for transfers between devices, local(): lax.all_to_all(first_old, 'ep', split_axis=0, concat_axis=0, tiled=True)  10.7 us
  transfers between devices with their start and end apart: 8, of which 7 were waited for; matrix products, arithmetic and copies ran while one was open for 14% of the time, Pallas kernels for 0%

commit v1 on v0

v1 whole, which is shorter than its diff:
```python
import functools

import jax
import jax.numpy as jnp
from jax import lax
from jax.experimental import pallas as pl
from jax.experimental.pallas import tpu as pltpu
from jax.sharding import PartitionSpec as P

beta_one = 0.9
beta_two = 0.95
bias_one = 0.9999734386011124
bias_two = 0.994079470779666
decay_rate = 0.1
adam_eps = 1e-08

LANES = 128
SUB = 8
MESH = pl.DeviceIdType.MESH
BF = jnp.bfloat16
F32 = jnp.float32


def splits(rows):
    first = 32 if rows > 32 else rows
    return [(0, first)] + ([(first, rows - first)] if rows > first else [])


def kernel(groups, owners, *refs):
    (acts_ref, grad_ref, counts_ref, p_ref, f_ref, s_ref, old_ref, rep_ref, new_ref) = refs[:9]
    step_ref, first_ref, second_ref = refs[9:12]
    rest = list(refs[12:])
    acts_all, p_v, f_v, s_v, st, st_in, pick, placed, step_v, first_v, second_v = rest[:11]
    rest = rest[11:]
    parts, rows, hidden = p_ref.shape
    cols = hidden // LANES
    tokens = acts_ref.shape[0]
    half = tokens // 2
    chunks = splits(rows)
    n_chunks = len(chunks)
    g_buf, gs, gi, os_, oi = (rest[i * n_chunks : (i + 1) * n_chunks] for i in range(5))
    rest = rest[5 * n_chunks :]
    (load_sem, g_sem, ring_send, ring_recv, pair_send, pair_recv, a_send, st_sem, gr_sem, out_sem) = rest

    r = lax.axis_index("edp")
    e = lax.axis_index("ep")
    chips = groups // 2
    core = lax.rem(r, 2)
    z = r // 2

    barrier = pltpu.get_barrier_semaphore()

    def greet_group(k, _):
        pl.semaphore_signal(
            barrier, inc=1, device_id=(lax.rem(r + k, groups), e), device_id_type=MESH
        )
        return 0

    def greet_owner(k, _):
        pl.semaphore_signal(
            barrier, inc=1, device_id=(r, lax.rem(e + k, owners)), device_id_type=MESH
        )
        return 0

    lax.fori_loop(1, groups, greet_group, 0)
    lax.fori_loop(1, owners, greet_owner, 0)

    own_acts = acts_all.at[r]
    load_acts = pltpu.make_async_copy(acts_ref, own_acts, load_sem.at[0])
    load_p = pltpu.make_async_copy(p_ref, p_v, load_sem.at[1])
    load_f = pltpu.make_async_copy(f_ref, f_v, load_sem.at[2])
    load_s = pltpu.make_async_copy(s_ref, s_v, load_sem.at[3])
    load_acts.start()
    load_p.start()
    load_f.start()
    load_s.start()

    load_acts.wait()
    token = lax.broadcasted_iota(jnp.int32, (half, hidden), 0)
    for slot in range(2):
        block = acts_all[r, slot * half : (slot + 1) * half, :].astype(F32)
        live = jnp.where(token < counts_ref[slot], block, 0.0)
        acts_all[r, slot * half : (slot + 1) * half, :] = live.astype(BF)

    pl.semaphore_wait(barrier, groups - 1 + owners - 1)

    def send_rows(i):
        first, size = chunks[i]
        lanes = pl.ds(pl.multiple_of(r * LANES, LANES), LANES)

        def body(k, _):
            to = lax.rem(r + k, groups)
            pltpu.make_async_remote_copy(
                src_ref=grad_ref.at[to, :, first : first + size, :],
                dst_ref=g_buf[i].at[:, :, lanes],
                send_sem=a_send.at[i],
                recv_sem=g_sem.at[i],
                device_id=(to, e),
                device_id_type=MESH,
            ).start()
            return 0

        lax.fori_loop(1, groups, body, 0)
        pltpu.make_async_copy(
            grad_ref.at[r, :, first : first + size, :], g_buf[i].at[:, :, lanes], g_sem.at[i]
        ).start()

    def ring(direction, hop, h):
        away = hop if direction == 0 else chips - hop
        block = lax.rem(z + chips - away, chips) * 2 + core
        to = lax.rem(z + (1 if direction == 0 else chips - 1), chips) * 2 + core
        ref = acts_all.at[block, pl.ds(h * half, half), :]
        return pltpu.make_async_remote_copy(
            src_ref=ref,
            dst_ref=ref,
            send_sem=ring_send.at[direction, hop, h],
            recv_sem=ring_recv.at[direction, hop, h],
            device_id=(to, e),
            device_id_type=MESH,
        )

    def arrived(direction, hop, h):
        away = hop + 1 if direction == 0 else chips - hop - 1
        block = lax.rem(z + chips - away, chips) * 2 + core
        ref = acts_all.at[block, pl.ds(h * half, half), :]
        return ref, pltpu.make_async_copy(ref, ref, ring_recv.at[direction, hop, h])

    def to_pair(ref):
        pltpu.make_async_remote_copy(
            src_ref=ref,
            dst_ref=ref,
            send_sem=pair_send,
            recv_sem=pair_recv,
            device_id=(r + 1 - 2 * core, e),
            device_id_type=MESH,
        ).start()

    far = chips // 2

    def goes(direction, hop, h):
        return hop < far - 1 or (hop == far - 1 and h == direction)

    ring_ops = [
        (direction, hop, h)
        for hop in range(far)
        for h in (0, 1)
        for direction in (0, 1)
        if goes(direction, hop, h)
    ]

    def spread(buf, landing, send_sem, recv_sem):
        def body(k, _):
            to = lax.rem(e + k, owners)
            pltpu.make_async_remote_copy(
                src_ref=buf.at[to],
                dst_ref=landing.at[e],
                send_sem=send_sem,
                recv_sem=recv_sem,
                device_id=(r, to),
                device_id_type=MESH,
            ).start()
            return 0

        lax.fori_loop(1, owners, body, 0)
        pltpu.make_async_copy(buf.at[e], landing.at[e], recv_sem).start()

    def wait_all(ref, sem):
        pltpu.make_async_copy(ref, ref, sem).wait()

    send_rows(0)
    for op in ring_ops:
        if op[1] == 0:
            ring(*op).start()
    to_pair(own_acts)

    load_p.wait()
    load_f.wait()
    load_s.wait()
    for q in range(parts):
        for c in range(cols):
            lanes = slice(c * LANES, (c + 1) * LANES)
            st[q * cols + c, 0] = p_v[q, :, lanes].astype(BF)
            st[q * cols + c, 1] = f_v[q, :, lanes]
            st[q * cols + c, 2] = s_v[q, :, lanes]
    spread(st, st_in, st_sem.at[0], st_sem.at[1])

    wide = SUB * owners
    lane = lax.broadcasted_iota(jnp.int32, (SUB, wide), 1)
    sub = lax.broadcasted_iota(jnp.int32, (SUB, wide), 0)
    same_row = lax.rem(lane, SUB) == sub
    lane_expert = lane // SUB
    old_wide = jnp.zeros((SUB, wide), jnp.int32)
    rep_wide = jnp.zeros((SUB, wide), jnp.int32)
    for i in range(owners):
        old_wide = jnp.where(lane_expert == i, old_ref[i], old_wide)
        rep_wide = jnp.where(lane_expert == i, rep_ref[i], rep_wide)
    for d in range(owners):
        at = slice(d * SUB, (d + 1) * SUB)
        pick[at, :wide] = jnp.where(same_row & (old_wide == new_ref[d]), 1.0, 0.0)
        pick[at, wide:] = jnp.where(same_row & (rep_wide == new_ref[d]), 1.0, 0.0)

    for direction, hop, h in ring_ops:
        ref, copy = arrived(direction, hop, h)
        copy.wait()
        if hop + 1 < far and goes(direction, hop + 1, h):
            ring(direction, hop + 1, h).start()
        to_pair(ref)
    for i in range(1, n_chunks):
        send_rows(i)
    for direction, hop, h in ring_ops:
        ring(direction, hop, h).wait_send()
    mine = acts_all.at[pl.ds(0, chips)]
    wait_all(mine, pair_recv)

    def gradients(i):
        first, size = chunks[i]
        wait_all(g_buf[i], g_sem.at[i])
        width = groups * LANES
        block = g_buf[i][...].astype(F32).reshape(parts * size, width)
        in_own = lax.rem(lax.broadcasted_iota(jnp.int32, block.shape, 1), LANES) < LANES // 2
        left = jnp.concatenate(
            [jnp.where(in_own, block, 0.0).astype(BF), jnp.where(in_own, 0.0, block).astype(BF)], 0
        )
        for c0 in range(0, hidden, 256):
            n = min(256, hidden - c0)
            right = acts_all[:, :, c0 : c0 + n].reshape(groups * tokens, n)
            out = jnp.dot(left, right, preferred_element_type=F32)
            for slot in range(2):
                for q in range(parts):
                    at = (slot * parts + q) * size
                    for c in range(n // LANES):
                        piece = out[at : at + size, c * LANES : (c + 1) * LANES]
                        gs[i][q * cols + c0 // LANES + c, slot] = piece.astype(BF)
        spread(gs[i], gi[i], gr_sem.at[0, i], gr_sem.at[1, i])

    for i in range(n_chunks):
        gradients(i)

    def stack(ref, item, at):
        return ref[:, item, at : at + SUB, :].astype(F32).reshape(wide, LANES).astype(BF)

    wait_all(st_in, st_sem.at[1])
    move = pick[:, :wide].astype(BF)
    for t in range(rows // SUB):
        state = jnp.concatenate([stack(st_in, item, t * SUB) for item in range(3)], 1)
        placed[t] = jnp.dot(move, state, preferred_element_type=F32)

    def update(i):
        first, size = chunks[i]
        wait_all(gi[i], gr_sem.at[1, i])
        both = pick[...].astype(BF)
        for t in range(size // SUB):
            at = t * SUB
            terms = jnp.concatenate([stack(gi[i], 0, at), stack(gi[i], 1, at)], 0)
            gradient = jnp.dot(both, terms, preferred_element_type=F32)
            old = placed[first // SUB + t]
            weights, first_old, second_old = (old[:, k * LANES : (k + 1) * LANES] for k in range(3))
            first_new = beta_one * first_old + (1.0 - beta_one) * gradient
            second_new = beta_two * second_old + (1.0 - beta_two) * gradient * gradient
            scaled = first_new / bias_one / (jnp.sqrt(second_new / bias_two) + adam_eps)
            step = -(scaled + decay_rate * weights)
            for item, value in enumerate((step, first_new, second_new)):
                os_[i][:, item, at : at + SUB, :] = value.reshape(owners, SUB, LANES).astype(BF)
        spread(os_[i], oi[i], out_sem.at[0, i], out_sem.at[1, i])

    for i in range(n_chunks):
        update(i)

    for i in range(n_chunks):
        first, size = chunks[i]
        wait_all(oi[i], out_sem.at[1, i])
        at = slice(first, first + size)
        for q in range(parts):
            for c in range(cols):
                lanes = slice(c * LANES, (c + 1) * LANES)
                step_v[q, at, lanes] = oi[i][q * cols + c, 0].astype(F32)
                first_v[q, at, lanes] = oi[i][q * cols + c, 1]
                second_v[q, at, lanes] = oi[i][q * cols + c, 2]
    stores = [
        pltpu.make_async_copy(a, b, load_sem.at[k])
        for k, (a, b) in enumerate(
            ((step_v, step_ref), (first_v, first_ref), (second_v, second_ref))
        )
    ]
    for s in stores:
        s.start()

    wait_all(mine, pair_send)
    others = pl.ds(0, owners - 1)
    wait_all(st.at[others], st_sem.at[0])
    for i in range(n_chunks):
        wait_all(g_buf[i].at[:, :, pl.ds(0, (groups - 1) * LANES)], a_send.at[i])
        wait_all(gs[i].at[others], gr_sem.at[0, i])
        wait_all(os_[i].at[others], out_sem.at[0, i])
    for s in stores:
        s.wait()


def local(groups, owners, token_acts, out_grad, counts, params, first, second, old, rep, new):
    model_width, width = out_grad.shape[2:]
    slot_count, tok, hidden = token_acts.shape[2:]
    row_count = model_width // groups
    cols = hidden // LANES
    parts = owners // cols
    rows = row_count // parts
    chunks = splits(rows)
    block = (parts, rows, hidden)
    any_spec = pl.BlockSpec(memory_space=pl.ANY)
    smem = pl.BlockSpec(memory_space=pltpu.SMEM)
    n = len(chunks)
    wide = SUB * owners
    dma = pltpu.SemaphoreType.DMA
    out = pl.pallas_call(
        functools.partial(kernel, groups, owners),
        out_shape=[
            jax.ShapeDtypeStruct(block, F32),
            jax.ShapeDtypeStruct(block, BF),
            jax.ShapeDtypeStruct(block, BF),
        ],
        in_specs=[any_spec, any_spec, smem, any_spec, any_spec, any_spec, smem, smem, smem],
        out_specs=[any_spec] * 3,
        scratch_shapes=[
            pltpu.VMEM((groups, slot_count * tok, hidden), BF),
            pltpu.VMEM(block, F32),
            pltpu.VMEM(block, BF),
            pltpu.VMEM(block, BF),
            pltpu.VMEM((owners, 3, rows, LANES), BF),
            pltpu.VMEM((owners, 3, rows, LANES), BF),
            pltpu.VMEM((wide, 2 * wide), F32),
            pltpu.VMEM((rows // SUB, wide, 3 * LANES), F32),
            pltpu.VMEM(block, F32),
            pltpu.VMEM(block, BF),
            pltpu.VMEM(block, BF),
        ]
        + [pltpu.VMEM((parts, size, groups * LANES), BF) for _, size in chunks]
        + [pltpu.VMEM((owners, 2, size, LANES), BF) for _, size in chunks] * 2
        + [pltpu.VMEM((owners, 3, size, LANES), BF) for _, size in chunks] * 2
        + [
            dma((4,)),
            dma((n,)),
            dma((2, groups // 4, 2)),
            dma((2, groups // 4, 2)),
            dma,
            dma,
            dma((n,)),
            dma((2,)),
            dma((2, n)),
            dma((2, n)),
        ],
        compiler_params=pltpu.CompilerParams(
            collective_id=0, has_side_effects=True, vmem_limit_bytes=48 * 1024 * 1024
        ),
    )(
        token_acts.reshape(slot_count * tok, hidden),
        out_grad.reshape(groups, parts, rows, width),
        counts.reshape(slot_count),
        params.reshape(block),
        first.reshape(block),
        second.reshape(block),
        old,
        rep,
        new,
    )
    return tuple(x.reshape(1, row_count, hidden) for x in out)


def solution(mesh):
    return jax.shard_map(
        functools.partial(local, mesh.shape["edp"], mesh.shape["ep"]),
        mesh=mesh,
        in_specs=(
            P("edp", "ep", None, None, None),
            P("edp", "ep", None, None),
            P("edp", "ep", None),
            P("ep", "edp", None),
            P("ep", "edp", None),
            P("ep", "edp", None),
            P(),
            P(),
            P(),
        ),
        out_specs=(P("ep", "edp", None), P("ep", "edp", None), P("ep", "edp", None)),
        check_vma=False,
    )
```

time: 282 us -> 121 us (0.43)
  Pallas kernels: 0 us -> 110 us
  waiting for transfers between devices: 94.3 us -> 0 us
  blocking collectives: 66.8 us -> 0 us
  starting transfers between devices: 43.4 us -> 0 us
  other arithmetic: 28.2 us -> 0 us
  local copies, waits for them, and re-layouts: 28.2 us -> 8.47 us
  between operations: 14.3 us -> 0.68 us
  matrix products: 4.96 us -> 0 us
    pallas_call x0 -> x1, Pallas kernels: none -> 110 us  [local(): pl.pallas_call(functools.partial(kernel, groups, owners), out_shape=[jax....]
    all_to_all x7 -> x0, waiting for transfers between devices: 75.6 us -> none  [the longest x1 19.8 us: local(): lax.all_to_all(weights, 'ep', split_axis=0, concat_axis=0, tiled=True)]
    all_to_all x2 -> x0, blocking collectives: 66.8 us -> none  [the longest x1 41 us: local(): lax.all_to_all(masked.reshape(groups, row_count, slot_count * tok_slot),...]
    all_to_all x7 -> x0, starting transfers between devices: 43.4 us -> none  [the longest x1 9.78 us: local(): lax.all_to_all(second_old, 'ep', split_axis=0, concat_axis=0, tiled=True)]
    all_gather x1 -> x0, waiting for transfers between devices: 18 us -> none  [local(): arrived = lax.all_gather(token_acts[0], 'edp', axis=0, tiled=True)]
    all_to_all x6 -> x0, other arithmetic: 10.2 us -> none  [the longest x2 3.57 us: local(): lax.all_to_all(placed_second, 'ep', split_axis=0, concat_axis=0, tiled=True)]
    convert_element_type x4 -> x0, other arithmetic: 9.16 us -> none  [the longest x2 5.02 us: adam_update(): second_new.astype(jnp.bfloat16)]
    mul x3 -> x0, local copies, waits for them, and re-layouts: 6.67 us -> none  [the longest x1 2.56 us: adam_update(): beta_one * first_old.astype(jnp.float32) + (1.0 - beta_one) * gradient]
  transfers between devices with their start and end apart: 8 -> 0, of which waited for: 7 -> 0; matrix products, arithmetic and copies ran while one was open for 14% -> 0% of each run, Pallas kernels for 0% -> 0%
where the time goes in v1:
time: 121 us; the launch traced here: 120 us
  Pallas kernels  110 us (91%)
  local copies, waits for them, and re-layouts  8.47 us (7%)
    pallas_call x1, Pallas kernels, local(): pl.pallas_call(functools.partial(kernel, groups, owners), out_shape=[jax....  110 us
    unnamed x21, local copies, waits for them, and re-layouts  8.47 us

profile of v1, /device:TPU:6, one launch (start us, length us, event | category | flops | bytes accessed | tf_op | source)
XLA Modules:
  0.0 119.6 jit_solution(1720188500782127166)
XLA Ops:
  0.6 0.0 copy-start.8
  0.6 0.0 copy-start.5
  0.7 0.0 copy-start.6
  0.7 0.0 copy-start.7
  0.7 0.6 copy-done.8
  1.3 0.0 copy-done.5
  1.3 0.0 copy-done.6
  1.3 0.0 copy-done.7
  1.3 0.0 copy-start
  1.3 1.2 copy-done
  2.5 0.0 copy-start.1
  2.5 1.2 copy-done.1
  3.7 0.0 copy-start.2
  3.7 1.0 copy-done.2
  4.7 0.0 copy-start.3
  4.7 1.0 copy-done.3
  5.7 0.0 copy-start.4
  5.7 0.9 copy-done.4
  6.7 110.5 %shard_map.112 = (f32[4,56,1024]{2,1,0:T(8,128)S(1)}, bf16[4,56,1024]{2,1,0:T(8,128)(2,1)S(1)}, bf16[4,56,1024]{2,1,0:T(8,128)(2,1)S(1)}) custom-call(bf16[128,1024]{1,0:T(8,128)(2,1)S(1)} %bitcast.16, bf16[16,4,56,128]{3,2,1,0:T(8,128)(2,1)S(1)} %bitcast.10, s32[2]{0:T(128)S(1)} %bitcast.17, f32[4,56,1024]{2,1,0:T(8,128)S(1)} %bitcast.11, ...), custom_call_target="tpu_custom_call" | custom-call | tf_op jit(solution)/shard_map/pallas_call | solution.py:313
  117.2 0.9 copy.15
  118.1 0.8 copy.16
  118.9 0.8 copy.17
Async XLA Ops:
  0.6 0.7 copy-start.8
  0.6 0.7 copy-start.5
  0.7 0.7 copy-start.6
  0.7 0.7 copy-start.7
  1.3 1.2 copy-start
  2.5 1.2 copy-start.1
  3.7 1.0 copy-start.2
  4.7 1.0 copy-start.3
  5.7 0.9 copy-start.4

commit v2 on v1

v2 whole, which is shorter than its diff:
```python
import functools

import jax
import jax.numpy as jnp
from jax import lax
from jax.experimental import pallas as pl
from jax.experimental.pallas import tpu as pltpu
from jax.sharding import PartitionSpec as P

beta_one = 0.9
beta_two = 0.95
bias_one = 0.9999734386011124
bias_two = 0.994079470779666
decay_rate = 0.1
adam_eps = 1e-08

LANES = 128
SUB = 8
MESH = pl.DeviceIdType.MESH
BF = jnp.bfloat16
F32 = jnp.float32


def splits(rows):
    first = 32 if rows > 32 else rows
    return [(0, first)] + ([(first, rows - first)] if rows > first else [])


def kernel(groups, owners, *refs):
    (acts_ref, grad_ref, counts_ref, p_ref, f_ref, s_ref, old_ref, rep_ref, new_ref) = refs[:9]
    n_chunks = len(splits(p_ref.shape[1]))
    new_p = refs[9]
    oi = refs[10 : 10 + n_chunks]
    rest = list(refs[10 + n_chunks :])
    acts_all, p_v, f_v, s_v, p_st, p_in, p_out, m_in, pick, placed = rest[:10]
    rest = rest[10:]
    parts, rows, hidden = p_ref.shape
    cols = hidden // LANES
    tokens = acts_ref.shape[0]
    half = tokens // 2
    chunks = splits(rows)
    g_buf, gs, gi, os_ = (rest[i * n_chunks : (i + 1) * n_chunks] for i in range(4))
    rest = rest[4 * n_chunks :]
    (load_sem, g_sem, ring_send, ring_recv, pair_sem, rows_send, p_sem, m_sem, new_sem, gr_sem, out_sem) = rest

    r = lax.axis_index("edp")
    e = lax.axis_index("ep")
    chips = groups // 2
    core = lax.rem(r, 2)
    z = r // 2

    load_acts = pltpu.make_async_copy(acts_ref, acts_all.at[r], load_sem.at[0])
    load_p = pltpu.make_async_copy(p_ref, p_v, load_sem.at[1])
    load_f = pltpu.make_async_copy(f_ref, f_v, load_sem.at[2])
    load_s = pltpu.make_async_copy(s_ref, s_v, load_sem.at[3])
    load_acts.start()
    load_p.start()
    load_f.start()
    load_s.start()

    barrier = pltpu.get_barrier_semaphore()

    def greet_group(k, _):
        pl.semaphore_signal(
            barrier, inc=1, device_id=(lax.rem(r + k, groups), e), device_id_type=MESH
        )
        return 0

    def greet_owner(k, _):
        pl.semaphore_signal(
            barrier, inc=1, device_id=(r, lax.rem(e + k, owners)), device_id_type=MESH
        )
        return 0

    lax.fori_loop(1, owners, greet_owner, 0)
    lax.fori_loop(1, groups, greet_group, 0)

    load_acts.wait()
    token = lax.broadcasted_iota(jnp.int32, (half, hidden), 0)
    for slot in range(2):
        block = acts_all[r, slot * half : (slot + 1) * half, :].astype(F32)
        live = jnp.where(token < counts_ref[slot], block, 0.0)
        acts_all[r, slot * half : (slot + 1) * half, :] = live.astype(BF)
    load_p.wait()
    for q in range(parts):
        for c in range(cols):
            p_st[q * cols + c] = p_v[q, :, c * LANES : (c + 1) * LANES].astype(BF)
    load_f.wait()
    load_s.wait()

    pl.semaphore_wait(barrier, groups - 1 + owners - 1)

    def send_rows(i):
        first, size = chunks[i]
        lanes = pl.ds(pl.multiple_of(r * LANES, LANES), LANES)

        def body(k, _):
            to = lax.rem(r + k, groups)
            pltpu.make_async_remote_copy(
                src_ref=grad_ref.at[to, :, first : first + size, :],
                dst_ref=g_buf[i].at[:, :, lanes],
                send_sem=rows_send.at[i],
                recv_sem=g_sem.at[i],
                device_id=(to, e),
                device_id_type=MESH,
            ).start()
            return 0

        lax.fori_loop(1, groups, body, 0)
        pltpu.make_async_copy(
            grad_ref.at[r, :, first : first + size, :], g_buf[i].at[:, :, lanes], g_sem.at[i]
        ).start()

    def ring(direction, hop, h):
        away = hop if direction == 0 else chips - hop
        block = lax.rem(z + chips - away, chips) * 2 + core
        to = lax.rem(z + (1 if direction == 0 else chips - 1), chips) * 2 + core
        ref = acts_all.at[block, pl.ds(h * half, half), :]
        return pltpu.make_async_remote_copy(
            src_ref=ref,
            dst_ref=ref,
            send_sem=ring_send.at[direction, hop, h],
            recv_sem=ring_recv.at[direction, hop, h],
            device_id=(to, e),
            device_id_type=MESH,
        )

    def arrived(direction, hop, h):
        away = hop + 1 if direction == 0 else chips - hop - 1
        block = lax.rem(z + chips - away, chips) * 2 + core
        ref = acts_all.at[block, pl.ds(h * half, half), :]
        return ref, pltpu.make_async_copy(ref, ref, ring_recv.at[direction, hop, h])

    def to_pair(ref):
        pltpu.make_async_remote_copy(
            src_ref=ref,
            dst_ref=ref,
            send_sem=pair_sem.at[0],
            recv_sem=pair_sem.at[1],
            device_id=(r + 1 - 2 * core, e),
            device_id_type=MESH,
        ).start()

    far = chips // 2

    def goes(direction, hop, h):
        return hop < far - 1 or (hop == far - 1 and h == direction)

    ring_ops = [
        (direction, hop, h)
        for hop in range(far)
        for h in (0, 1)
        for direction in (0, 1)
        if goes(direction, hop, h)
    ]

    def spread(source, landing, sems):
        def body(k, _):
            to = lax.rem(e + k, owners)
            pltpu.make_async_remote_copy(
                src_ref=source(to),
                dst_ref=landing,
                send_sem=sems.at[0],
                recv_sem=sems.at[1],
                device_id=(r, to),
                device_id_type=MESH,
            ).start()
            return 0

        lax.fori_loop(1, owners, body, 0)
        pltpu.make_async_copy(source(e), landing, sems.at[1]).start()

    def block_of(ref):
        def at(j):
            lanes = pl.ds(pl.multiple_of(lax.rem(j, cols) * LANES, LANES), LANES)
            return ref.at[j // cols, :, lanes]

        return at

    def wait_all(ref, sem):
        pltpu.make_async_copy(ref, ref, sem).wait()

    for op in ring_ops:
        if op[1] == 0:
            ring(*op).start()
    spread(lambda j: p_st.at[j], p_in.at[e], p_sem)
    to_pair(acts_all.at[r])
    send_rows(0)
    spread(block_of(f_v), m_in.at[e, 0], m_sem)
    spread(block_of(s_v), m_in.at[e, 1], m_sem)

    wide = SUB * owners
    lane = lax.broadcasted_iota(jnp.int32, (SUB, wide), 1)
    sub = lax.broadcasted_iota(jnp.int32, (SUB, wide), 0)
    same_row = lax.rem(lane, SUB) == sub
    lane_expert = lane // SUB
    old_wide = jnp.zeros((SUB, wide), jnp.int32)
    rep_wide = jnp.zeros((SUB, wide), jnp.int32)
    for i in range(owners):
        old_wide = jnp.where(lane_expert == i, old_ref[i], old_wide)
        rep_wide = jnp.where(lane_expert == i, rep_ref[i], rep_wide)
    for d in range(owners):
        at = slice(d * SUB, (d + 1) * SUB)
        pick[at, :wide] = jnp.where(same_row & (old_wide == new_ref[d]), 1.0, 0.0)
        pick[at, wide:] = jnp.where(same_row & (rep_wide == new_ref[d]), 1.0, 0.0)

    def stack(block):
        return block.astype(F32).reshape(wide, LANES).astype(BF)

    def pass_on():
        wait_all(p_in, p_sem.at[1])
        move = pick[:, :wide].astype(BF)
        for t in range(rows // SUB):
            at = slice(t * SUB, (t + 1) * SUB)
            moved = jnp.dot(move, stack(p_in[:, at, :]), preferred_element_type=F32)
            p_out[:, at, :] = moved.reshape(owners, SUB, LANES).astype(BF)
        spread(lambda j: p_out.at[j], new_p.at[e], new_sem)

    for hop in range(far):
        for op in ring_ops:
            if op[1] != hop:
                continue
            direction, _, h = op
            ref, copy = arrived(*op)
            copy.wait()
            if hop + 1 < far and goes(direction, hop + 1, h):
                ring(direction, hop + 1, h).start()
            to_pair(ref)
        if hop == min(1, far - 1):
            pass_on()
        if hop == max(0, far - 2):
            for i in range(1, n_chunks):
                send_rows(i)
    for op in ring_ops:
        ring(*op).wait_send()
    mine = acts_all.at[pl.ds(0, chips)]
    wait_all(mine, pair_sem.at[1])

    def gradients(i):
        first, size = chunks[i]
        wait_all(g_buf[i], g_sem.at[i])
        width = groups * LANES
        block = g_buf[i][...].astype(F32).reshape(parts * size, width)
        in_own = lax.rem(lax.broadcasted_iota(jnp.int32, block.shape, 1), LANES) < LANES // 2
        left = jnp.concatenate(
            [jnp.where(in_own, block, 0.0).astype(BF), jnp.where(in_own, 0.0, block).astype(BF)], 0
        )
        for c0 in range(0, hidden, 256):
            n = min(256, hidden - c0)
            right = acts_all[:, :, c0 : c0 + n].reshape(groups * tokens, n)
            out = jnp.dot(left, right, preferred_element_type=F32)
            for slot in range(2):
                for q in range(parts):
                    at = (slot * parts + q) * size
                    for c in range(n // LANES):
                        piece = out[at : at + size, c * LANES : (c + 1) * LANES]
                        gs[i][q * cols + c0 // LANES + c, slot] = piece.astype(BF)
        spread(lambda j: gs[i].at[j], gi[i].at[e], gr_sem.at[i])

    def place():
        wait_all(m_in, m_sem.at[1])
        move = pick[:, :wide].astype(BF)
        for t in range(rows // SUB):
            at = slice(t * SUB, (t + 1) * SUB)
            both = jnp.concatenate([stack(m_in[:, item, at, :]) for item in range(2)], 1)
            placed[t] = jnp.dot(move, both, preferred_element_type=F32)

    def update(i):
        first, size = chunks[i]
        wait_all(gi[i], gr_sem.at[i, 1])
        both = pick[...].astype(BF)
        for t in range(size // SUB):
            at = slice(t * SUB, (t + 1) * SUB)
            terms = jnp.concatenate([stack(gi[i][:, item, at, :]) for item in range(2)], 0)
            gradient = jnp.dot(both, terms, preferred_element_type=F32)
            old = placed[first // SUB + t]
            first_old, second_old = old[:, :LANES], old[:, LANES:]
            first_new = beta_one * first_old + (1.0 - beta_one) * gradient
            second_new = beta_two * second_old + (1.0 - beta_two) * gradient * gradient
            for item, value in enumerate((first_new, second_new)):
                os_[i][:, item, at, :] = value.reshape(owners, SUB, LANES).astype(BF)
        spread(lambda j: os_[i].at[j], oi[i].at[e], out_sem.at[i])

    gradients(0)
    place()
    for i in range(1, n_chunks):
        gradients(i)
    for i in range(n_chunks):
        update(i)

    others = pl.ds(0, owners - 1)
    wait_all(mine, pair_sem.at[0])
    wait_all(p_st.at[others], p_sem.at[0])
    wait_all(m_in.at[others], m_sem.at[0])
    wait_all(p_out.at[others], new_sem.at[0])
    wait_all(new_p, new_sem.at[1])
    for i in range(n_chunks):
        wait_all(g_buf[i].at[:, :, pl.ds(0, (groups - 1) * LANES)], rows_send.at[i])
        wait_all(gs[i].at[others], gr_sem.at[i, 0])
        wait_all(os_[i].at[others], out_sem.at[i, 0])
        wait_all(oi[i], out_sem.at[i, 1])


def finish(chunks, p_ref, *refs):
    n = len(chunks)
    step_ref, first_ref, second_ref = refs[n:]
    for c in range(p_ref.shape[0]):
        lanes = slice(c * LANES, (c + 1) * LANES)
        for i, (first, size) in enumerate(chunks):
            at = slice(first, first + size)
            first_new, second_new = refs[i][c, 0], refs[i][c, 1]
            weights = p_ref[c, at, :].astype(F32)
            scaled = (first_new.astype(F32) / bias_one) / (
                jnp.sqrt(second_new.astype(F32) / bias_two) + adam_eps
            )
            step_ref[0, at, lanes] = -(scaled + decay_rate * weights)
            first_ref[0, at, lanes] = first_new
            second_ref[0, at, lanes] = second_new


def local(groups, owners, token_acts, out_grad, counts, params, first, second, old, rep, new):
    model_width, width = out_grad.shape[2:]
    slot_count, tok, hidden = token_acts.shape[2:]
    row_count = model_width // groups
    cols = hidden // LANES
    parts = owners // cols
    rows = row_count // parts
    chunks = splits(rows)
    block = (parts, rows, hidden)
    hbm = pl.BlockSpec(memory_space=pl.ANY)
    smem = pl.BlockSpec(memory_space=pltpu.SMEM)
    n = len(chunks)
    wide = SUB * owners
    dma = pltpu.SemaphoreType.DMA
    landed = pl.pallas_call(
        functools.partial(kernel, groups, owners),
        out_shape=[jax.ShapeDtypeStruct((owners, rows, LANES), BF)]
        + [jax.ShapeDtypeStruct((owners, 2, size, LANES), BF) for _, size in chunks],
        in_specs=[hbm, hbm, smem, hbm, hbm, hbm, smem, smem, smem],
        out_specs=[hbm] * (1 + n),
        scratch_shapes=[
            pltpu.VMEM((groups, slot_count * tok, hidden), BF),
            pltpu.VMEM(block, F32),
            pltpu.VMEM(block, BF),
            pltpu.VMEM(block, BF),
            pltpu.VMEM((owners, rows, LANES), BF),
            pltpu.VMEM((owners, rows, LANES), BF),
            pltpu.VMEM((owners, rows, LANES), BF),
            pltpu.VMEM((owners, 2, rows, LANES), BF),
            pltpu.VMEM((wide, 2 * wide), F32),
            pltpu.VMEM((rows // SUB, wide, 2 * LANES), F32),
        ]
        + [pltpu.VMEM((parts, size, groups * LANES), BF) for _, size in chunks]
        + [pltpu.VMEM((owners, 2, size, LANES), BF) for _, size in chunks] * 3
        + [
            dma((4,)),
            dma((n,)),
            dma((2, groups // 4, 2)),
            dma((2, groups // 4, 2)),
            dma((2,)),
            dma((n,)),
            dma((2,)),
            dma((2,)),
            dma((2,)),
            dma((n, 2)),
            dma((n, 2)),
        ],
        compiler_params=pltpu.CompilerParams(
            collective_id=0, has_side_effects=True, vmem_limit_bytes=60 * 1024 * 1024
        ),
    )(
        token_acts.reshape(slot_count * tok, hidden),
        out_grad.reshape(groups, parts, rows, width),
        counts.reshape(slot_count),
        params.reshape(block),
        first.reshape(block),
        second.reshape(block),
        old,
        rep,
        new,
    )
    out_block = pl.BlockSpec((1, rows, hidden), lambda q: (q, 0, 0))
    out = pl.pallas_call(
        functools.partial(finish, chunks),
        grid=(parts,),
        out_shape=[
            jax.ShapeDtypeStruct(block, F32),
            jax.ShapeDtypeStruct(block, BF),
            jax.ShapeDtypeStruct(block, BF),
        ],
        in_specs=[pl.BlockSpec((cols, rows, LANES), lambda q: (q, 0, 0))]
        + [pl.BlockSpec((cols, 2, size, LANES), lambda q: (q, 0, 0, 0)) for _, size in chunks],
        out_specs=[out_block] * 3,
    )(*landed)
    return tuple(x.reshape(1, row_count, hidden) for x in out)


def solution(mesh):
    return jax.shard_map(
        functools.partial(local, mesh.shape["edp"], mesh.shape["ep"]),
        mesh=mesh,
        in_specs=(
            P("edp", "ep", None, None, None),
            P("edp", "ep", None, None),
            P("edp", "ep", None),
            P("ep", "edp", None),
            P("ep", "edp", None),
            P("ep", "edp", None),
            P(),
            P(),
            P(),
        ),
        out_specs=(P("ep", "edp", None), P("ep", "edp", None), P("ep", "edp", None)),
        check_vma=False,
    )
```

time: 121 us -> 105 us (0.87)
  local copies, waits for them, and re-layouts: 8.47 us -> 0 us
  Pallas kernels: 110 us -> 103 us
    pallas_call x1, Pallas kernels: 110 us -> 99.1 us  [local(): pl.pallas_call(functools.partial(kernel, groups, owners), out_shape=[jax....]
    unnamed x21 -> x0, local copies, waits for them, and re-layouts: 8.47 us -> none
    pallas_call x0 -> x1, Pallas kernels: none -> 3.77 us  [local(): pl.pallas_call(functools.partial(finish, chunks), grid=(parts,), out_shap...]
where the time goes in v2:
time: 105 us; the launch traced here: 104 us
  Pallas kernels  103 us (98%)
    pallas_call x1, Pallas kernels, local(): pl.pallas_call(functools.partial(kernel, groups, owners), out_shape=[jax....  99.1 us
    pallas_call x1, Pallas kernels, local(): pl.pallas_call(functools.partial(finish, chunks), grid=(parts,), out_shap...  3.77 us

profile of v2, /device:TPU:6, one launch (start us, length us, event | category | flops | bytes accessed | tf_op | source)
XLA Modules:
  0.0 103.6 jit_solution(9735067224746825981)
XLA Ops:
  0.6 99.1 %shard_map.112 = (bf16[32,56,128]{2,1,0:T(8,128)(2,1)}, bf16[32,2,32,128]{3,2,1,0:T(8,128)(2,1)}, bf16[32,2,24,128]{3,2,1,0:T(8,128)(2,1)}) custom-call(bf16[128,1024]{1,0:T(8,128)(2,1)} %bitcast.13, bf16[16,4,56,128]{3,2,1,0:T(8,128)(2,1)} %bitcast.9, s32[2]{0:T(128)} %bitcast.14, f32[4,56,1024]{2,1,0:T(8,128)} %bitcast.10, bf16[4,56,1024]{2,1,0:T(8,128)(2,1)} %bitcast.11, ...), custom_call_target="tpu_custom_call" | custom-call | tf_op jit(solution)/shard_map/pallas_call | solution.py:335
  99.8 3.8 %shard_map.113 = (f32[4,56,1024]{2,1,0:T(8,128)}, bf16[4,56,1024]{2,1,0:T(8,128)(2,1)}, bf16[4,56,1024]{2,1,0:T(8,128)(2,1)}) custom-call(bf16[32,56,128]{2,1,0:T(8,128)(2,1)} %get-tuple-element.9.p_ref, bf16[32,2,32,128]{3,2,1,0:T(8,128)(2,1)} %get-tuple-element.10.refs_0_, bf16[32,2,24,128]{3,2,1,0:T(8,128)(2,1)} %get-tuple-element.11.refs_1_), custom_call_target="tpu_custom_call" | custom-call | tf_op jit(solution)/shard_map/pallas_call | solution.py:383

commit v3 on v2

--- a/solution.py
+++ b/solution.py
@@ -22,18 +22,19 @@
 
 
 def splits(rows):
-    first = 32 if rows > 32 else rows
-    return [(0, first)] + ([(first, rows - first)] if rows > first else [])
+    first = rows // SUB * 3 // 7 * SUB
+    return [(0, first), (first, rows - first)] if first else [(0, rows)]
 
 
 def kernel(groups, owners, *refs):
-    (acts_ref, grad_ref, counts_ref, p_ref, f_ref, s_ref, old_ref, rep_ref, new_ref) = refs[:9]
+    (acts_ref, grad_ref, counts_hbm, p_ref, f_ref, s_ref, old_hbm, rep_hbm, new_hbm) = refs[:9]
     n_chunks = len(splits(p_ref.shape[1]))
     new_p = refs[9]
     oi = refs[10 : 10 + n_chunks]
     rest = list(refs[10 + n_chunks :])
-    acts_all, p_v, f_v, s_v, p_st, p_in, p_out, m_in, pick, placed = rest[:10]
-    rest = rest[10:]
+    counts_ref, old_ref, rep_ref, new_ref = rest[:4]
+    acts_all, p_v, f_v, s_v, p_st, p_in, p_out, m_in, pick, placed = rest[4:14]
+    rest = rest[14:]
     parts, rows, hidden = p_ref.shape
     cols = hidden // LANES
     tokens = acts_ref.shape[0]
@@ -49,11 +50,19 @@
     core = lax.rem(r, 2)
     z = r // 2
 
+    load_index = [
+        pltpu.make_async_copy(a, b, load_sem.at[4 + k])
+        for k, (a, b) in enumerate(
+            ((counts_hbm, counts_ref), (old_hbm, old_ref), (rep_hbm, rep_ref), (new_hbm, new_ref))
+        )
+    ]
     load_acts = pltpu.make_async_copy(acts_ref, acts_all.at[r], load_sem.at[0])
     load_p = pltpu.make_async_copy(p_ref, p_v, load_sem.at[1])
     load_f = pltpu.make_async_copy(f_ref, f_v, load_sem.at[2])
     load_s = pltpu.make_async_copy(s_ref, s_v, load_sem.at[3])
     load_acts.start()
+    for copy in load_index:
+        copy.start()
     load_p.start()
     load_f.start()
     load_s.start()
@@ -76,6 +85,8 @@
     lax.fori_loop(1, groups, greet_group, 0)
 
     load_acts.wait()
+    for copy in load_index:
+        copy.wait()
     token = lax.broadcasted_iota(jnp.int32, (half, hidden), 0)
     for slot in range(2):
         block = acts_all[r, slot * half : (slot + 1) * half, :].astype(F32)
@@ -303,19 +314,29 @@
 
 def finish(chunks, p_ref, *refs):
     n = len(chunks)
-    step_ref, first_ref, second_ref = refs[n:]
-    for c in range(p_ref.shape[0]):
-        lanes = slice(c * LANES, (c + 1) * LANES)
-        for i, (first, size) in enumerate(chunks):
-            at = slice(first, first + size)
-            first_new, second_new = refs[i][c, 0], refs[i][c, 1]
-            weights = p_ref[c, at, :].astype(F32)
-            scaled = (first_new.astype(F32) / bias_one) / (
-                jnp.sqrt(second_new.astype(F32) / bias_two) + adam_eps
-            )
-            step_ref[0, at, lanes] = -(scaled + decay_rate * weights)
-            first_ref[0, at, lanes] = first_new
-            second_ref[0, at, lanes] = second_new
+    step_ref, first_ref, second_ref, step_v, first_v, second_v, sems = refs[n:]
+    parts, _, hidden = step_v.shape
+    cols = hidden // LANES
+    copies = []
+    for q in range(parts):
+        for c in range(cols):
+            lanes = slice(c * LANES, (c + 1) * LANES)
+            for i, (first, size) in enumerate(chunks):
+                at = slice(first, first + size)
+                first_new, second_new = refs[i][q * cols + c, 0], refs[i][q * cols + c, 1]
+                weights = p_ref[q * cols + c, at, :].astype(F32)
+                root = jnp.sqrt(second_new.astype(F32) * (bias_one * bias_one / bias_two))
+                scaled = first_new.astype(F32) / (root + bias_one * adam_eps)
+                step_v[q, at, lanes] = -(scaled + decay_rate * weights)
+                first_v[q, at, lanes] = first_new
+                second_v[q, at, lanes] = second_new
+        for k, (a, b) in enumerate(
+            ((step_v, step_ref), (first_v, first_ref), (second_v, second_ref))
+        ):
+            copies.append(pltpu.make_async_copy(a.at[q], b.at[q], sems.at[k, q]))
+            copies[-1].start()
+    for copy in copies:
+        copy.wait()
 
 
 def local(groups, owners, token_acts, out_grad, counts, params, first, second, old, rep, new):
@@ -327,18 +348,33 @@
     rows = row_count // parts
     chunks = splits(rows)
     block = (parts, rows, hidden)
-    hbm = pl.BlockSpec(memory_space=pl.ANY)
-    smem = pl.BlockSpec(memory_space=pltpu.SMEM)
+    hbm = pl.BlockSpec(memory_space=pltpu.HBM)
+    vmem = pl.BlockSpec(memory_space=pltpu.VMEM)
     n = len(chunks)
     wide = SUB * owners
     dma = pltpu.SemaphoreType.DMA
+    operands = (
+        token_acts.reshape(slot_count * tok, hidden),
+        out_grad.reshape(groups, parts, rows, width),
+        counts.reshape(slot_count),
+        params.reshape(block),
+        first.reshape(block),
+        second.reshape(block),
+        old,
+        rep,
+        new,
+    )
     landed = pl.pallas_call(
         functools.partial(kernel, groups, owners),
         out_shape=[jax.ShapeDtypeStruct((owners, rows, LANES), BF)]
         + [jax.ShapeDtypeStruct((owners, 2, size, LANES), BF) for _, size in chunks],
-        in_specs=[hbm, hbm, smem, hbm, hbm, hbm, smem, smem, smem],
-        out_specs=[hbm] * (1 + n),
+        in_specs=[hbm] * len(operands),
+        out_specs=[vmem] * (1 + n),
         scratch_shapes=[
+            pltpu.SMEM((slot_count,), jnp.int32),
+            pltpu.SMEM((owners,), jnp.int32),
+            pltpu.SMEM((owners,), jnp.int32),
+            pltpu.SMEM((owners,), jnp.int32),
             pltpu.VMEM((groups, slot_count * tok, hidden), BF),
             pltpu.VMEM(block, F32),
             pltpu.VMEM(block, BF),
@@ -353,7 +389,7 @@
         + [pltpu.VMEM((parts, size, groups * LANES), BF) for _, size in chunks]
         + [pltpu.VMEM((owners, 2, size, LANES), BF) for _, size in chunks] * 3
         + [
-            dma((4,)),
+            dma((8,)),
             dma((n,)),
             dma((2, groups // 4, 2)),
             dma((2, groups // 4, 2)),
@@ -366,31 +402,27 @@
             dma((n, 2)),
         ],
         compiler_params=pltpu.CompilerParams(
-            collective_id=0, has_side_effects=True, vmem_limit_bytes=60 * 1024 * 1024
+            collective_id=0, has_side_effects=True, vmem_limit_bytes=36 * 1024 * 1024
         ),
     )(
-        token_acts.reshape(slot_count * tok, hidden),
-        out_grad.reshape(groups, parts, rows, width),
-        counts.reshape(slot_count),
-        params.reshape(block),
-        first.reshape(block),
-        second.reshape(block),
-        old,
-        rep,
-        new,
+        *(pltpu.with_memory_space_constraint(v, pltpu.HBM) for v in operands)
     )
-    out_block = pl.BlockSpec((1, rows, hidden), lambda q: (q, 0, 0))
     out = pl.pallas_call(
         functools.partial(finish, chunks),
-        grid=(parts,),
         out_shape=[
             jax.ShapeDtypeStruct(block, F32),
             jax.ShapeDtypeStruct(block, BF),
             jax.ShapeDtypeStruct(block, BF),
         ],
-        in_specs=[pl.BlockSpec((cols, rows, LANES), lambda q: (q, 0, 0))]
-        + [pl.BlockSpec((cols, 2, size, LANES), lambda q: (q, 0, 0, 0)) for _, size in chunks],
-        out_specs=[out_block] * 3,
+        in_specs=[vmem] * (1 + n),
+        out_specs=[pl.BlockSpec(memory_space=pltpu.HBM)] * 3,
+        scratch_shapes=[
+            pltpu.VMEM(block, F32),
+            pltpu.VMEM(block, BF),
+            pltpu.VMEM(block, BF),
+            dma((3, parts)),
+        ],
+        compiler_params=pltpu.CompilerParams(vmem_limit_bytes=16 * 1024 * 1024),
     )(*landed)
     return tuple(x.reshape(1, row_count, hidden) for x in out)
 

time: 105 us -> 99.8 us (0.950); the launches traced: 104 us -> 99.6 us
  Pallas kernels: 103 us -> 99 us
    pallas_call x1, Pallas kernels: 3.77 us -> 1.49 us  [local(): pl.pallas_call(functools.partial(finish, chunks), out_shape=[jax.ShapeDty...]
    pallas_call x1, Pallas kernels: 99.1 us -> 97.5 us  [local(): pl.pallas_call(functools.partial(kernel, groups, owners), out_shape=[jax....]
where the time goes in v3:
time: 99.8 us; the launch traced here: 99.6 us
  Pallas kernels  99 us (99%)
    pallas_call x1, Pallas kernels, local(): pl.pallas_call(functools.partial(kernel, groups, owners), out_shape=[jax....  97.5 us

profile of v3, /device:TPU:6, one launch (start us, length us, event | category | flops | bytes accessed | tf_op | source)
XLA Modules:
  0.0 99.6 jit_solution(13292553978447774000)
XLA Ops:
  0.6 97.5 %shard_map.112 = (bf16[32,56,128]{2,1,0:T(8,128)(2,1)S(1)}, bf16[32,2,24,128]{3,2,1,0:T(8,128)(2,1)S(1)}, bf16[32,2,32,128]{3,2,1,0:T(8,128)(2,1)S(1)}) custom-call(bf16[128,1024]{1,0:T(8,128)(2,1)} %bitcast.13, bf16[16,4,56,128]{3,2,1,0:T(8,128)(2,1)} %bitcast.9, s32[2]{0:T(128)} %bitcast.14, f32[4,56,1024]{2,1,0:T(8,128)} %bitcast.10, ...), custom_call_target="tpu_custom_call" | custom-call | tf_op jit(solution)/shard_map/pallas_call | solution.py:367
  98.1 1.5 %shard_map.113 = (f32[4,56,1024]{2,1,0:T(8,128)}, bf16[4,56,1024]{2,1,0:T(8,128)(2,1)}, bf16[4,56,1024]{2,1,0:T(8,128)(2,1)}) custom-call(bf16[32,56,128]{2,1,0:T(8,128)(2,1)S(1)} %get-tuple-element.9.p_ref, bf16[32,2,24,128]{3,2,1,0:T(8,128)(2,1)S(1)} %get-tuple-element.10.refs_0_, bf16[32,2,32,128]{3,2,1,0:T(8,128)(2,1)S(1)} %get-tuple-element.11.refs_1_), custom_call_target="tpu_custom_call" | custom-call | tf_op jit(solution)/shard_map/pallas_call | solution.py:410

commit v4 on v3

--- a/solution.py
+++ b/solution.py
@@ -26,12 +26,27 @@
     return [(0, first), (first, rows - first)] if first else [(0, rows)]
 
 
+def finish_part(chunk, q, cols, p_ref, moments_ref, results, row):
+    first, size = chunk
+    step, first_out, second_out = results
+    at = slice(row, row + size)
+    for c in range(cols):
+        lanes = slice(c * LANES, (c + 1) * LANES)
+        first_new, second_new = moments_ref[q * cols + c, 0], moments_ref[q * cols + c, 1]
+        weights = p_ref[q * cols + c, first : first + size, :].astype(F32)
+        root = jnp.sqrt(second_new.astype(F32) * (bias_one * bias_one / bias_two))
+        scaled = first_new.astype(F32) / (root + bias_one * adam_eps)
+        step[q, at, lanes] = -(scaled + decay_rate * weights)
+        first_out[q, at, lanes] = first_new
+        second_out[q, at, lanes] = second_new
+
+
 def kernel(groups, owners, *refs):
     (acts_ref, grad_ref, counts_hbm, p_ref, f_ref, s_ref, old_hbm, rep_hbm, new_hbm) = refs[:9]
     n_chunks = len(splits(p_ref.shape[1]))
     new_p = refs[9]
-    oi = refs[10 : 10 + n_chunks]
-    rest = list(refs[10 + n_chunks :])
+    results = refs[11:14]
+    rest = list(refs[14:])
     counts_ref, old_ref, rep_ref, new_ref = rest[:4]
     acts_all, p_v, f_v, s_v, p_st, p_in, p_out, m_in, pick, placed = rest[4:14]
     rest = rest[14:]
@@ -41,7 +56,8 @@
     half = tokens // 2
     chunks = splits(rows)
     g_buf, gs, gi, os_ = (rest[i * n_chunks : (i + 1) * n_chunks] for i in range(4))
-    rest = rest[4 * n_chunks :]
+    oi = rest[4 * n_chunks : 5 * n_chunks - 1] + [refs[10]]
+    rest = rest[5 * n_chunks - 1 :]
     (load_sem, g_sem, ring_send, ring_recv, pair_sem, rows_send, p_sem, m_sem, new_sem, gr_sem, out_sem) = rest
 
     r = lax.axis_index("edp")
@@ -49,6 +65,23 @@
     chips = groups // 2
     core = lax.rem(r, 2)
     z = r // 2
+
+    barrier = pltpu.get_barrier_semaphore()
+
+    def greet_group(k, _):
+        pl.semaphore_signal(
+            barrier, inc=1, device_id=(lax.rem(r + k, groups), e), device_id_type=MESH
+        )
+        return 0
+
+    def greet_owner(k, _):
+        pl.semaphore_signal(
+            barrier, inc=1, device_id=(r, lax.rem(e + k, owners)), device_id_type=MESH
+        )
+        return 0
+
+    lax.fori_loop(1, owners, greet_owner, 0)
+    lax.fori_loop(1, groups, greet_group, 0)
 
     load_index = [
         pltpu.make_async_copy(a, b, load_sem.at[4 + k])
@@ -67,23 +100,6 @@
     load_f.start()
     load_s.start()
 
-    barrier = pltpu.get_barrier_semaphore()
-
-    def greet_group(k, _):
-        pl.semaphore_signal(
-            barrier, inc=1, device_id=(lax.rem(r + k, groups), e), device_id_type=MESH
-        )
-        return 0
-
-    def greet_owner(k, _):
-        pl.semaphore_signal(
-            barrier, inc=1, device_id=(r, lax.rem(e + k, owners)), device_id_type=MESH
-        )
-        return 0
-
-    lax.fori_loop(1, owners, greet_owner, 0)
-    lax.fori_loop(1, groups, greet_group, 0)
-
     load_acts.wait()
     for copy in load_index:
         copy.wait()
@@ -191,10 +207,10 @@
     def wait_all(ref, sem):
         pltpu.make_async_copy(ref, ref, sem).wait()
 
+    spread(lambda j: p_st.at[j], p_in.at[e], p_sem)
     for op in ring_ops:
         if op[1] == 0:
             ring(*op).start()
-    spread(lambda j: p_st.at[j], p_in.at[e], p_sem)
     to_pair(acts_all.at[r])
     send_rows(0)
     spread(block_of(f_v), m_in.at[e, 0], m_sem)
@@ -299,44 +315,44 @@
     for i in range(n_chunks):
         update(i)
 
+    wait_all(new_p, new_sem.at[1])
+    for i in range(n_chunks - 1):
+        wait_all(oi[i], out_sem.at[i, 1])
+        for q in range(parts):
+            finish_part(chunks[i], q, cols, new_p, oi[i], results, chunks[i][0])
+
     others = pl.ds(0, owners - 1)
     wait_all(mine, pair_sem.at[0])
     wait_all(p_st.at[others], p_sem.at[0])
     wait_all(m_in.at[others], m_sem.at[0])
     wait_all(p_out.at[others], new_sem.at[0])
-    wait_all(new_p, new_sem.at[1])
     for i in range(n_chunks):
         wait_all(g_buf[i].at[:, :, pl.ds(0, (groups - 1) * LANES)], rows_send.at[i])
         wait_all(gs[i].at[others], gr_sem.at[i, 0])
         wait_all(os_[i].at[others], out_sem.at[i, 0])
-        wait_all(oi[i], out_sem.at[i, 1])
-
-
-def finish(chunks, p_ref, *refs):
-    n = len(chunks)
-    step_ref, first_ref, second_ref, step_v, first_v, second_v, sems = refs[n:]
-    parts, _, hidden = step_v.shape
-    cols = hidden // LANES
+    wait_all(oi[n_chunks - 1], out_sem.at[n_chunks - 1, 1])
+
+
+def finish(chunk, p_ref, moments_ref, *refs):
+    done, outs, last, sems = refs[:3], refs[3:6], refs[6:9], refs[9]
+    first, size = chunk
+    parts, _, hidden = done[0].shape
     copies = []
+
+    def copy(k, q, source, rows):
+        target = outs[k].at[:, rows, :] if q == parts else outs[k].at[q, rows, :]
+        copies.append(pltpu.make_async_copy(source, target, sems.at[k, q]))
+        copies[-1].start()
+
+    if first:
+        for k in range(3):
+            copy(k, parts, done[k].at[:, pl.ds(0, first), :], pl.ds(0, first))
     for q in range(parts):
-        for c in range(cols):
-            lanes = slice(c * LANES, (c + 1) * LANES)
-            for i, (first, size) in enumerate(chunks):
-                at = slice(first, first + size)
-                first_new, second_new = refs[i][q * cols + c, 0], refs[i][q * cols + c, 1]
-                weights = p_ref[q * cols + c, at, :].astype(F32)
-                root = jnp.sqrt(second_new.astype(F32) * (bias_one * bias_one / bias_two))
-                scaled = first_new.astype(F32) / (root + bias_one * adam_eps)
-                step_v[q, at, lanes] = -(scaled + decay_rate * weights)
-                first_v[q, at, lanes] = first_new
-                second_v[q, at, lanes] = second_new
-        for k, (a, b) in enumerate(
-            ((step_v, step_ref), (first_v, first_ref), (second_v, second_ref))
-        ):
-            copies.append(pltpu.make_async_copy(a.at[q], b.at[q], sems.at[k, q]))
-            copies[-1].start()
-    for copy in copies:
-        copy.wait()
+        finish_part(chunk, q, hidden // LANES, p_ref, moments_ref, last, 0)
+        for k in range(3):
+            copy(k, q, last[k].at[q], pl.ds(first, size))
+    for started in copies:
+        started.wait()
 
 
 def local(groups, owners, token_acts, out_grad, counts, params, first, second, old, rep, new):
@@ -367,9 +383,10 @@
     landed = pl.pallas_call(
         functools.partial(kernel, groups, owners),
         out_shape=[jax.ShapeDtypeStruct((owners, rows, LANES), BF)]
-        + [jax.ShapeDtypeStruct((owners, 2, size, LANES), BF) for _, size in chunks],
+        + [jax.ShapeDtypeStruct((owners, 2, chunks[-1][1], LANES), BF)]
+        + [jax.ShapeDtypeStruct(block, kind) for kind in (F32, BF, BF)],
         in_specs=[hbm] * len(operands),
-        out_specs=[vmem] * (1 + n),
+        out_specs=[vmem] * 5,
         scratch_shapes=[
             pltpu.SMEM((slot_count,), jnp.int32),
             pltpu.SMEM((owners,), jnp.int32),
@@ -388,6 +405,7 @@
         ]
         + [pltpu.VMEM((parts, size, groups * LANES), BF) for _, size in chunks]
         + [pltpu.VMEM((owners, 2, size, LANES), BF) for _, size in chunks] * 3
+        + [pltpu.VMEM((owners, 2, size, LANES), BF) for _, size in chunks[:-1]]
         + [
             dma((8,)),
             dma((n,)),
@@ -407,21 +425,13 @@
     )(
         *(pltpu.with_memory_space_constraint(v, pltpu.HBM) for v in operands)
     )
+    last = (parts, chunks[-1][1], hidden)
     out = pl.pallas_call(
-        functools.partial(finish, chunks),
-        out_shape=[
-            jax.ShapeDtypeStruct(block, F32),
-            jax.ShapeDtypeStruct(block, BF),
-            jax.ShapeDtypeStruct(block, BF),
-        ],
-        in_specs=[vmem] * (1 + n),
-        out_specs=[pl.BlockSpec(memory_space=pltpu.HBM)] * 3,
-        scratch_shapes=[
-            pltpu.VMEM(block, F32),
-            pltpu.VMEM(block, BF),
-            pltpu.VMEM(block, BF),
-            dma((3, parts)),
-        ],
+        functools.partial(finish, chunks[-1]),
+        out_shape=[jax.ShapeDtypeStruct(block, kind) for kind in (F32, BF, BF)],
+        in_specs=[vmem] * 5,
+        out_specs=[hbm] * 3,
+        scratch_shapes=[pltpu.VMEM(last, kind) for kind in (F32, BF, BF)] + [dma((3, parts + 1))],
         compiler_params=pltpu.CompilerParams(vmem_limit_bytes=16 * 1024 * 1024),
     )(*landed)
     return tuple(x.reshape(1, row_count, hidden) for x in out)

time: 99.8 us -> 99.7 us (level)
  no operation moved by 1% of the time
where the time goes in v4:
time: 99.7 us; the launch traced here: 99.5 us
  Pallas kernels  98.8 us (99%)
    pallas_call x1, Pallas kernels, local(): pl.pallas_call(functools.partial(kernel, groups, owners), out_shape=[jax....  97.5 us

profile of v4, /device:TPU:6, one launch (start us, length us, event | category | flops | bytes accessed | tf_op | source)
XLA Modules:
  0.0 99.5 jit_solution(13747388432493613249)
XLA Ops:
  0.6 97.5 %shard_map.112 = (bf16[32,56,128]{2,1,0:T(8,128)(2,1)S(1)}, bf16[32,2,32,128]{3,2,1,0:T(8,128)(2,1)S(1)}, f32[4,56,1024]{2,1,0:T(8,128)S(1)}, bf16[4,56,1024]{2,1,0:T(8,128)(2,1)S(1)}, bf16[4,56,1024]{2,1,0:T(8,128)(2,1)S(1)}) custom-call(bf16[128,1024]{1,0:T(8,128)(2,1)} %bitcast.13, bf16[16,4,56,128]{3,2,1,0:T(8,128)(2,1)} %bitcast.9, s32[2]{0:T(128)} %bitcast.14, ...), custom_call_target="tpu_custom_call" | custom-call | tf_op jit(solution)/shard_map/pallas_call | solution.py:383
  98.1 1.3 %shard_map.113 = (f32[4,56,1024]{2,1,0:T(8,128)}, bf16[4,56,1024]{2,1,0:T(8,128)(2,1)}, bf16[4,56,1024]{2,1,0:T(8,128)(2,1)}) custom-call(bf16[32,56,128]{2,1,0:T(8,128)(2,1)S(1)} %get-tuple-element.11.p_ref, bf16[32,2,32,128]{3,2,1,0:T(8,128)(2,1)S(1)} %get-tuple-element.12.moments_ref, f32[4,56,1024]{2,1,0:T(8,128)S(1)} %get-tuple-element.13.refs_0_, ...), custom_call_target="tpu_custom_call" | custom-call | tf_op jit(solution)/shard_map/pallas_call | solution.py:429

commit v5 on v4

--- a/solution.py
+++ b/solution.py
@@ -48,8 +48,8 @@
     results = refs[11:14]
     rest = list(refs[14:])
     counts_ref, old_ref, rep_ref, new_ref = rest[:4]
-    acts_all, p_v, f_v, s_v, p_st, p_in, p_out, m_in, pick, placed = rest[4:14]
-    rest = rest[14:]
+    acts_all, p_v, f_v, s_v, p_st, p_in, p_out, m_in, m_st, pick, placed = rest[4:15]
+    rest = rest[15:]
     parts, rows, hidden = p_ref.shape
     cols = hidden // LANES
     tokens = acts_ref.shape[0]
@@ -80,8 +80,10 @@
         )
         return 0
 
-    lax.fori_loop(1, owners, greet_owner, 0)
-    lax.fori_loop(1, groups, greet_group, 0)
+    for k in range(1, owners):
+        greet_owner(k, 0)
+    for k in range(1, groups):
+        greet_group(k, 0)
 
     load_index = [
         pltpu.make_async_copy(a, b, load_sem.at[4 + k])
@@ -114,6 +116,11 @@
             p_st[q * cols + c] = p_v[q, :, c * LANES : (c + 1) * LANES].astype(BF)
     load_f.wait()
     load_s.wait()
+    for q in range(parts):
+        for c in range(cols):
+            lanes = slice(c * LANES, (c + 1) * LANES)
+            m_st[q * cols + c, 0] = f_v[q, :, lanes]
+            m_st[q * cols + c, 1] = s_v[q, :, lanes]
 
     pl.semaphore_wait(barrier, groups - 1 + owners - 1)
 
@@ -197,13 +204,6 @@
         lax.fori_loop(1, owners, body, 0)
         pltpu.make_async_copy(source(e), landing, sems.at[1]).start()
 
-    def block_of(ref):
-        def at(j):
-            lanes = pl.ds(pl.multiple_of(lax.rem(j, cols) * LANES, LANES), LANES)
-            return ref.at[j // cols, :, lanes]
-
-        return at
-
     def wait_all(ref, sem):
         pltpu.make_async_copy(ref, ref, sem).wait()
 
@@ -213,8 +213,7 @@
             ring(*op).start()
     to_pair(acts_all.at[r])
     send_rows(0)
-    spread(block_of(f_v), m_in.at[e, 0], m_sem)
-    spread(block_of(s_v), m_in.at[e, 1], m_sem)
+    spread(lambda j: m_st.at[j], m_in.at[e], m_sem)
 
     wide = SUB * owners
     lane = lax.broadcasted_iota(jnp.int32, (SUB, wide), 1)
@@ -400,6 +399,7 @@
             pltpu.VMEM((owners, rows, LANES), BF),
             pltpu.VMEM((owners, rows, LANES), BF),
             pltpu.VMEM((owners, 2, rows, LANES), BF),
+            pltpu.VMEM((owners, 2, rows, LANES), BF),
             pltpu.VMEM((wide, 2 * wide), F32),
             pltpu.VMEM((rows // SUB, wide, 2 * LANES), F32),
         ]

time: 99.7 us -> 99.6 us (level)
  no operation moved by 1% of the time
where the time goes in v5:
time: 99.6 us; the launch traced here: 99.2 us
  Pallas kernels  98.6 us (99%)
    pallas_call x1, Pallas kernels, local(): pl.pallas_call(functools.partial(kernel, groups, owners), out_shape=[jax....  97.2 us

profile of v5, /device:TPU:6, one launch (start us, length us, event | category | flops | bytes accessed | tf_op | source)
XLA Modules:
  0.0 99.2 jit_solution(7476929057490815173)
XLA Ops:
  0.6 97.2 %shard_map.112 = (bf16[32,56,128]{2,1,0:T(8,128)(2,1)S(1)}, bf16[32,2,32,128]{3,2,1,0:T(8,128)(2,1)S(1)}, f32[4,56,1024]{2,1,0:T(8,128)S(1)}, bf16[4,56,1024]{2,1,0:T(8,128)(2,1)S(1)}, bf16[4,56,1024]{2,1,0:T(8,128)(2,1)S(1)}) custom-call(bf16[128,1024]{1,0:T(8,128)(2,1)} %bitcast.13, bf16[16,4,56,128]{3,2,1,0:T(8,128)(2,1)} %bitcast.9, s32[2]{0:T(128)} %bitcast.14, ...), custom_call_target="tpu_custom_call" | custom-call | tf_op jit(solution)/shard_map/pallas_call | solution.py:382
  97.9 1.3 %shard_map.113 = (f32[4,56,1024]{2,1,0:T(8,128)}, bf16[4,56,1024]{2,1,0:T(8,128)(2,1)}, bf16[4,56,1024]{2,1,0:T(8,128)(2,1)}) custom-call(bf16[32,56,128]{2,1,0:T(8,128)(2,1)S(1)} %get-tuple-element.11.p_ref, bf16[32,2,32,128]{3,2,1,0:T(8,128)(2,1)S(1)} %get-tuple-element.12.moments_ref, f32[4,56,1024]{2,1,0:T(8,128)S(1)} %get-tuple-element.13.refs_0_, ...), custom_call_target="tpu_custom_call" | custom-call | tf_op jit(solution)/shard_map/pallas_call | solution.py:429
